TPU v7x, 32 devices: a whole 2x2x4 slice. The times are simulated.
32 devices in a mesh: groups: 2 (over x), fsdp: 2 (over core), rows: 8 (over z, y).
Axes of the slice: x: 2, y: 2, z: 4, core: 2. Of those that a mesh axis runs over, the one named last changes fastest.
Arguments:
- tokens: bfloat16 [4, 128, 16, 1024], P(('groups', 'fsdp'), 'rows'), parts along dimension 0, may hold values from -6 to 6
- cell_mask: int32 [4, 128, 16], P(('groups', 'fsdp'), 'rows'), parts along dimension 0, may hold values 0 or 1
- shifts: int32 [2], replicated, may hold values from 1 to 15
- projection_in: bfloat16 [1024, 1536], P(('fsdp', 'rows')), may hold values from -2 to 2
- projection_out: bfloat16 [512, 1024], P(('fsdp', 'rows')), may hold values from -0.25 to 0.25
- cotangent: bfloat16 [4, 128, 16, 1024], P(('groups', 'fsdp'), 'rows'), parts along dimension 0, may hold values from -6 to 6
Outputs:
- output: bfloat16 [4, 128, 16, 1024], P(('groups', 'fsdp'), 'rows'), parts along dimension 0
- grad_tokens: bfloat16 [4, 128, 16, 1024], P(('groups', 'fsdp'), 'rows'), parts along dimension 0
- projection_in_grad: float32 [2048, 1536], P(('groups', 'fsdp', 'rows')), parts along dimension 0
- projection_out_grad: float32 [1024, 1024], P(('groups', 'fsdp', 'rows')), parts along dimension 0
There are 2 independent parts, one for each index of `groups`. A program takes and returns all parts, laid end to end along the dimension named above; an argument that names none is the same for every part. Nothing has to cross between parts.
All inputs are finite; a program needn't handle non-finite values. No bound on the sum of `cell_mask` on one device may be relied on, other than what follows from the above.
Results may differ from a plain program's by a relative error of at most 0.011.
Values may be sent and summed in bfloat16 or wider, within the bound.
No kernel may reach another device: no remote copies, remote signals or barrier semaphores. Data moves between devices by JAX's collectives and lax.ppermute only.
A program may use at most 64 MiB of HBM per device.

v0:
```python
import jax
import jax.numpy as jnp
from jax import lax
from jax.sharding import PartitionSpec as P

HEADS = 8
HD = 64
WIN = 16


def shifted(block, axis, distance):
    devices = range(lax.axis_size(axis))
    route = [((i - distance) % len(devices), i) for i in devices]
    return lax.ppermute(block, axis, route)


def roll_columns(grid_field, offset):
    col_count = grid_field.shape[1]
    doubled = jnp.concatenate([grid_field, grid_field], axis=1)
    return lax.dynamic_slice_in_dim(doubled, offset, col_count, 1)


def into_windows(grid_field):
    row_count, col_count, channels = grid_field.shape
    blocks = grid_field.reshape(row_count // WIN, WIN, col_count // WIN, WIN, channels)
    return blocks.transpose(0, 2, 1, 3, 4).reshape(-1, WIN * WIN, channels)


def from_windows(windowed, row_count, col_count):
    channels = windowed.shape[-1]
    blocks = windowed.reshape(row_count // WIN, col_count // WIN, WIN, WIN, channels)
    return blocks.transpose(0, 2, 1, 3, 4).reshape(row_count, col_count, channels)


def normalize(values_f32):
    mean_value = jnp.mean(values_f32, axis=-1, keepdims=True)
    centered = values_f32 - mean_value
    variance = jnp.mean(centered * centered, axis=-1, keepdims=True)
    inv_std = lax.rsqrt(variance + 1e-05)
    return (centered * inv_std, inv_std)


def body(tokens, cell_mask, shifts, projection_in, projection_out, cotangent):
    row_count = tokens.shape[1]
    col_count = tokens.shape[2]
    model_dim = tokens.shape[3]
    hidden_width = HEADS * HD
    score_scale = HD ** (-0.5)
    grid_rows = row_count * lax.axis_size("rows")
    shift_row = shifts[0]
    shift_col = shifts[1]
    full_in, full_out = (
        lax.all_gather(projection_in, ("fsdp", "rows"), axis=0, tiled=True),
        lax.all_gather(projection_out, ("fsdp", "rows"), axis=0, tiled=True),
    )
    mask_wire = cell_mask.astype(jnp.bfloat16)
    next_tokens, next_mask = shifted((tokens, mask_wire), "rows", -1)

    def to_slab(own_rows, next_rows):
        joined = jnp.concatenate([own_rows[0], next_rows[0]], axis=0)
        return roll_columns(lax.dynamic_slice_in_dim(joined, shift_row, row_count, 0), shift_col)

    def to_owner(slab_rows, prev_rows):
        joined = jnp.concatenate([prev_rows, slab_rows], axis=0)
        return lax.dynamic_slice_in_dim(joined, row_count - shift_row, row_count, 0)

    slab_tokens = to_slab(tokens, next_tokens)
    slab_mask = to_slab(mask_wire, next_mask)
    row_ids = (
        lax.axis_index("rows") * row_count + shift_row + jnp.arange(row_count, dtype=jnp.int32)
    ) % grid_rows
    col_ids = (jnp.arange(col_count, dtype=jnp.int32) + shift_col) % col_count
    region = (row_ids < shift_row).astype(jnp.int32)[:, None] * 2 + (col_ids < shift_col).astype(
        jnp.int32
    )[None, :]
    region_win = into_windows(region[:, :, None])[:, :, 0]
    mask_win = into_windows(slab_mask[:, :, None])[:, :, 0] > 0
    token_win = into_windows(slab_tokens)
    window_count = token_win.shape[0]
    window_len = token_win.shape[1]
    allowed = (region_win[:, :, None] == region_win[:, None, :]) & (
        mask_win[:, None, :] | jnp.eye(window_len, dtype=bool)[None]
    )
    normed, inv_std = normalize(token_win.astype(jnp.float32))
    normed_bf = normed.astype(jnp.bfloat16)
    flat_normed = normed_bf.reshape(-1, model_dim)
    packed_heads = jnp.dot(flat_normed, full_in, preferred_element_type=jnp.float32).astype(
        jnp.bfloat16
    )
    packed_heads = packed_heads.reshape(window_count, window_len, 3, HEADS, HD)
    query_heads = packed_heads[:, :, 0]
    key_heads = packed_heads[:, :, 1]
    value_heads = packed_heads[:, :, 2]
    scores = (
        jnp.einsum("wqhd,wkhd->whqk", query_heads, key_heads, preferred_element_type=jnp.float32)
        * score_scale
    )
    scores = jnp.where(allowed[:, None], scores, -1e30)
    row_peak = jnp.max(scores, axis=-1, keepdims=True)
    exp_terms = jnp.exp(scores - row_peak)
    attention = exp_terms / jnp.sum(exp_terms, axis=-1, keepdims=True)
    attention_bf = attention.astype(jnp.bfloat16)
    context = jnp.einsum(
        "whqk,wkhd->wqhd", attention_bf, value_heads, preferred_element_type=jnp.float32
    ).astype(jnp.bfloat16)
    context = context.reshape(window_count, window_len, hidden_width)
    slab_context = roll_columns(from_windows(context, row_count, col_count), col_count - shift_col)
    prev_context = shifted(slab_context, "rows", 1)
    own_context = to_owner(slab_context, prev_context)
    projected = jnp.dot(
        own_context.reshape(-1, hidden_width), full_out, preferred_element_type=jnp.float32
    )
    output = (
        tokens[0].astype(jnp.float32) + projected.reshape(row_count, col_count, model_dim)
    ).astype(jnp.bfloat16)
    next_cotangent = shifted(cotangent, "rows", -1)
    cot_win = into_windows(to_slab(cotangent, next_cotangent))
    flat_cot = cot_win.reshape(-1, model_dim)
    flat_context = context.reshape(-1, hidden_width)
    grad_context = lax.dot_general(
        flat_cot, full_out, (((1,), (1,)), ((), ())), preferred_element_type=jnp.float32
    ).astype(jnp.bfloat16)
    term_out = lax.dot_general(
        flat_context, flat_cot, (((0,), (0,)), ((), ())), preferred_element_type=jnp.float32
    )
    grad_heads = grad_context.reshape(window_count, window_len, HEADS, HD)
    grad_attention = jnp.einsum(
        "wqhd,wkhd->whqk", grad_heads, value_heads, preferred_element_type=jnp.float32
    )
    grad_scores = (
        attention
        * (grad_attention - jnp.sum(grad_attention * attention, axis=-1, keepdims=True))
        * score_scale
    ).astype(jnp.bfloat16)
    grad_query = jnp.einsum(
        "whqk,wkhd->wqhd", grad_scores, key_heads, preferred_element_type=jnp.float32
    )
    grad_key = jnp.einsum(
        "whqk,wqhd->wkhd", grad_scores, query_heads, preferred_element_type=jnp.float32
    )
    grad_value = jnp.einsum(
        "whqk,wqhd->wkhd", attention_bf, grad_heads, preferred_element_type=jnp.float32
    )
    grad_packed = (
        jnp.stack([grad_query, grad_key, grad_value], axis=2)
        .astype(jnp.bfloat16)
        .reshape(-1, 3 * hidden_width)
    )
    term_in = lax.dot_general(
        flat_normed, grad_packed, (((0,), (0,)), ((), ())), preferred_element_type=jnp.float32
    )
    grad_normed = lax.dot_general(
        grad_packed, full_in, (((1,), (1,)), ((), ())), preferred_element_type=jnp.float32
    )
    grad_normed = grad_normed.reshape(window_count, window_len, model_dim)
    grad_win = (
        cot_win.astype(jnp.float32)
        + inv_std
        * (
            grad_normed
            - jnp.mean(grad_normed, axis=-1, keepdims=True)
            - normed * jnp.mean(grad_normed * normed, axis=-1, keepdims=True)
        )
    ).astype(jnp.bfloat16)
    slab_grad = roll_columns(from_windows(grad_win, row_count, col_count), col_count - shift_col)
    prev_grad = shifted(slab_grad, "rows", 1)
    own_grad = to_owner(slab_grad, prev_grad)
    grad_in, grad_out = (
        lax.psum_scatter(term_in, ("fsdp", "rows"), scatter_dimension=0, tiled=True),
        lax.psum_scatter(term_out, ("fsdp", "rows"), scatter_dimension=0, tiled=True),
    )
    return (output[None], own_grad[None], grad_in, grad_out)


def solution(mesh):
    placed = (
        P(("groups", "fsdp"), "rows", None, None),
        P(("groups", "fsdp"), "rows", None),
        P(),
        P(("fsdp", "rows"), None),
        P(("fsdp", "rows"), None),
        P(("groups", "fsdp"), "rows", None, None),
    )
    return jax.shard_map(
        body,
        mesh=mesh,
        in_specs=placed,
        out_specs=(
            P(("groups", "fsdp"), "rows", None, None),
            P(("groups", "fsdp"), "rows", None, None),
            P(("groups", "fsdp", "rows"), None),
            P(("groups", "fsdp", "rows"), None),
        ),
        check_vma=False,
    )
```

profile of v0, /device:TPU:0, one launch (start us, length us, event | category | flops | bytes accessed | tf_op | source)
XLA Modules:
  0.0 278.8 jit_solution(13945911961746731159)
XLA Ops:
  7.2 0.7 all-gather.3.cloned.1.call-update
  8.0 0.7 convert_element_type.146
  8.7 6.0 %collective-permute-start.1 = (bf16[1,16,16]{2,1,0:T(8,128)(2,1)S(1)}, bf16[1,16,16]{2,1,0:T(8,128)(2,1)S(1)}, u32[]{:S(2)}, u32[]{:S(2)}) collective-permute-start(bf16[1,16,16]{2,1,0:T(8,128)(2,1)S(1)} %convert_element_type.146), channel_id=1, source_target_pairs={{1,0},{2,1},{3,2},{4,3},{5,4},{6,5},{7,6},{0,7},{9,8},{10,9},{11,1... | collective-permute-start | bytes 1544 | tf_op jit(solution)/shard_map/ppermute | solution.py:14
  14.7 0.5 collective-permute-start.3
  15.2 1.4 collective-permute-start
  16.7 0.7 convert_bitcast_fusion
  17.4 1.3 fusion.66
  18.7 0.7 compare_convert_fusion
  19.9 0.6 compare_select_fusion.4
  24.9 19.1 %collective-permute-done = bf16[1,16,16,1024]{3,2,1,0:T(8,128)(2,1)S(1)} collective-permute-done((bf16[1,16,16,1024]{3,2,1,0:T(8,128)(2,1)}, bf16[1,16,16,1024]{3,2,1,0:T(8,128)(2,1)S(1)}, u32[]{:S(2)}, u32[]{:S(2)}) %collective-permute-start) | collective-permute-done | bytes 524320 | tf_op jit(solution)/shard_map/ppermute | solution.py:14
  44.0 1.1 fusion.39
  46.9 22.2 %all-gather.3.cloned.1.call-done = bf16[1024,1536]{1,0:T(8,128)(2,1)} async-done(((bf16[64,1536]{1,0:T(8,128)(2,1)}), bf16[1024,1536]{1,0:T(8,128)(2,1)}) %all-gather.3.cloned.1.call-update) | async-done | bytes 3145744 | tf_op jit(solution)/shard_map/all_gather | solution.py:53
  69.1 3.8 %convolution_convert_fusion = bf16[256,1536]{1,0:T(8,128)(2,1)} fusion(bf16[256,1024]{1,0:T(8,128)(2,1)S(1)} %fusion.29, bf16[1024,1536]{1,0:T(8,128)(2,1)} %all-gather.3.cloned.1.call-done), kind=kOutput, calls=%fused_computation.2 | convolution fusion | flops 805699584 | bytes 4456448 | tf_op jit(solution)/shard_map/dot_general | solution.py:87
  72.9 1.4 copy.21
  74.3 2.2 fusion.67
  76.5 1.9 convolution_convert_fusion.2
  78.4 0.7 copy-done.2
  79.1 1.8 fusion.68
  80.9 27.2 %all-gather.5.cloned.1.call-done = bf16[512,1024]{1,0:T(8,128)(2,1)} async-done(((bf16[32,1024]{1,0:T(8,128)(2,1)}), bf16[512,1024]{1,0:T(8,128)(2,1)}) %all-gather.5.cloned.1.call-update) | async-done | bytes 1048592 | tf_op jit(solution)/shard_map/all_gather | solution.py:54
  108.1 1.7 convolution_convert_fusion.1
  110.0 1.8 fusion.49
  111.7 4.2 %fusion.14 = bf16[1,256,1,8,64]{1,4,3,2,0:T(8,128)(2,1)S(1)} fusion(f32[8,256,256]{1,2,0:T(8,128)} %fusion.49, bf16[1,256,3,8,64]{1,4,3,2,0:T(8,128)(2,1)S(1)} %bitcast.119, f32[8,256,256]{1,2,0:T(8,128)} %get-tuple-element.11, f32[8,256]{1,0:T(8,128)S(1)} %get-tuple-element.10), kind=kOutput, calls=%fused_computation.15 | convolution fusion | flops 70781184 | bytes 8929280 | tf_op jit(solution)/shard_map/whqk,wkhd->wqhd/dot_general | solution.py:135
  116.0 5.1 %fusion.17 = bf16[1,256,1,8,64]{1,4,3,2,0:T(8,128)(2,1)} fusion(f32[8,256,256]{1,2,0:T(8,128)} %fusion.49, bf16[1,256,3,8,64]{1,4,3,2,0:T(8,128)(2,1)S(1)} %bitcast.120, f32[8,256,256]{1,2,0:T(8,128)} %get-tuple-element.11, f32[8,256]{1,0:T(8,128)S(1)} %get-tuple-element.10), kind=kOutput, calls=%fused_computation.16 | convolution fusion | flops 70781184 | bytes 8929280 | tf_op jit(solution)/shard_map/whqk,wqhd->wkhd/dot_general | solution.py:138
  121.1 2.2 convolution_bitcast_fusion
  123.3 3.8 %fusion.31 = f32[1024,1536]{1,0:T(8,128)} fusion(bf16[256,1536]{0,1:T(8,128)(2,1)S(1)} %bitcast.112, f32[1,256,1,1,1,1,1024]{6,1,5,4,3,2,0:T(8,128)S(1)} %bitcast.109, f32[256]{0:T(256)S(1)} %add_rsqrt_fusion, f32[256]{0:T(256)S(1)} %div.24), kind=kOutput, calls=%fused_computation.50 | convolution fusion | flops 806092800 | bytes 8128512 | tf_op jit(solution)/shard_map/dot_general | solution.py:149
  129.2 3.1 %fusion.64 = (f32[256]{0:T(256)S(1)}, f32[256]{0:T(256)S(1)}, f32[256,1024]{1,0:T(8,128)S(1)}) fusion(f32[256]{0:T(256)S(1)} %add_rsqrt_fusion, f32[256]{0:T(256)S(1)} %div.24, bf16[16,16,1024]{2,1,0:T(8,128)(2,1)S(1)} %get-tuple-element.7, bf16[256,1536]{0,1:T(8,128)(2,1)S(1)} %bitcast.113, bf16[1024,1536]{1,0:T(8,128)(2,1)} %all-gather.3.cloned.1.call-done), kind=kOutput, calls=%fused_computation.106 | convolution fusion | flops 806878720 | bytes 5509120 | tf_op jit(solution)/shard_map/dot_general | solution.py:152
  133.9 1.5 collective-permute-start.2
  136.7 27.6 %collective-permute-done.2 = bf16[16,16,512]{2,1,0:T(8,128)(2,1)S(1)} collective-permute-done((bf16[16,16,512]{2,1,0:T(8,128)(2,1)S(1)}, bf16[16,16,512]{2,1,0:T(8,128)(2,1)S(1)}, u32[]{:S(2)}, u32[]{:S(2)}) %collective-permute-start.2) | collective-permute-done | bytes 262176 | tf_op jit(solution)/shard_map/ppermute | solution.py:14
  164.2 1.3 fusion.13
  165.5 1.0 fusion.34
  166.5 16.6 %reduce-scatter.5.cloned.1.call-done = f32[32,1024]{1,0:T(8,128)} async-done(((f32[512,1024]{1,0:T(8,128)}), f32[32,1024]{1,0:T(8,128)}) %reduce-scatter.5.cloned.1.call-update) | async-done | bytes 131088 | tf_op jit(solution)/shard_map/reduce_scatter | solution.py:170
  183.1 89.1 %reduce-scatter.3.cloned.1.call-done = f32[64,1536]{1,0:T(8,128)} async-done(((f32[1024,1536]{1,0:T(8,128)}), f32[64,1536]{1,0:T(8,128)}) %reduce-scatter.3.cloned.1.call-update) | async-done | bytes 393232 | tf_op jit(solution)/shard_map/reduce_scatter | solution.py:169
  (45 shorter events, 4.9 us)
Async XLA Ops:
  7.2 38.4 %copy-start.4 = (bf16[1,16,16,1024]{3,2,1,0:T(8,128)(2,1)S(1)}, bf16[1,16,16,1024]{3,2,1,0:T(8,128)(2,1)}, u32[]{:S(2)}) copy-start(bf16[1,16,16,1024]{3,2,1,0:T(8,128)(2,1)} %param.11) | copy-start | bytes 1572868
  7.2 61.9 %all-gather.3.cloned.1.call-start = ((), (), s32[]{:S(2)}) async-start(), calls=%async_computation.2 | async-start | bytes 3342336 | tf_op jit(solution)/shard_map/all_gather | solution.py:53
  7.9 100.2 %all-gather.5.cloned.1.call-start = ((), (), s32[]{:S(2)}) async-start(), calls=%async_computation.3 | async-start | bytes 1114112 | tf_op jit(solution)/shard_map/all_gather | solution.py:54
  8.7 15.8 %collective-permute-start.1 = (bf16[1,16,16]{2,1,0:T(8,128)(2,1)S(1)}, bf16[1,16,16]{2,1,0:T(8,128)(2,1)S(1)}, u32[]{:S(2)}, u32[]{:S(2)}) collective-permute-start(bf16[1,16,16]{2,1,0:T(8,128)(2,1)S(1)} %convert_element_type.146), channel_id=1, source_target_pairs={{1,0},{2,1},{3,2},{4,3},{5,4},{6,5},{7,6},{0,7},{9,8},{10,9},{11,1... | collective-permute-start | bytes 1544 | tf_op jit(solution)/shard_map/ppermute | solution.py:14
  14.7 30.9 %collective-permute-start.3 = (bf16[1,16,16,1024]{3,2,1,0:T(8,128)(2,1)}, bf16[1,16,16,1024]{3,2,1,0:T(8,128)(2,1)S(1)}, u32[]{:S(2)}, u32[]{:S(2)}) collective-permute-start(bf16[1,16,16,1024]{3,2,1,0:T(8,128)(2,1)} %param.11), channel_id=1, source_target_pairs={{1,0},{2,1},{3,2},{4,3},{5,4},{6,5},{7,6},{0,7},{9,8},{10,9},{11,1... | collective-permute-start | bytes 1572872 | tf_op jit(solution)/shard_map/ppermute | solution.py:14
  15.2 28.8 %collective-permute-start = (bf16[1,16,16,1024]{3,2,1,0:T(8,128)(2,1)}, bf16[1,16,16,1024]{3,2,1,0:T(8,128)(2,1)S(1)}, u32[]{:S(2)}, u32[]{:S(2)}) collective-permute-start(bf16[1,16,16,1024]{3,2,1,0:T(8,128)(2,1)} %param.6), channel_id=1, source_target_pairs={{1,0},{2,1},{3,2},{4,3},{5,4},{6,5},{7,6},{0,7},{9,8},{10,9},{11,1... | collective-permute-start | bytes 1572872 | tf_op jit(solution)/shard_map/ppermute | solution.py:14
  16.6 166.5 %reduce-scatter.5.cloned.1.call-start = ((), (), s32[]{:S(2)}) async-start(), calls=%async_computation.5 | async-start | bytes 2228224 | tf_op jit(solution)/shard_map/reduce_scatter | solution.py:170
  78.4 0.7 copy-start.2
  80.9 191.4 %reduce-scatter.3.cloned.1.call-start = ((), (), s32[]{:S(2)}) async-start(), calls=%async_computation.4 | async-start | bytes 6684672 | tf_op jit(solution)/shard_map/reduce_scatter | solution.py:169
  121.1 2.2 copy-start.5
  127.2 1.4 copy-start.3
  132.4 31.8 %copy-start = (bf16[512,1024]{1,0:T(8,128)(2,1)S(1)}, bf16[512,1024]{1,0:T(8,128)(2,1)}, u32[]{:S(2)}) copy-start(bf16[512,1024]{1,0:T(8,128)(2,1)} %all-gather.5.cloned.1.call-done) | copy-start | bytes 3145732
  132.4 31.8 %copy-start.1 = (bf16[1,16,16,1024]{3,2,1,0:T(8,128)(2,1)S(1)}, bf16[1,16,16,1024]{3,2,1,0:T(8,128)(2,1)}, u32[]{:S(2)}) copy-start(bf16[1,16,16,1024]{3,2,1,0:T(8,128)(2,1)} %param.6) | copy-start | bytes 1572868
  133.2 32.3 %collective-permute-start.4 = (bf16[16,16,1024]{2,1,0:T(8,128)(2,1)S(1)}, bf16[16,16,1024]{2,1,0:T(8,128)(2,1)S(1)}, u32[]{:S(2)}, u32[]{:S(2)}) collective-permute-start(bf16[16,16,1024]{2,1,0:T(8,128)(2,1)S(1)} %fusion.35), channel_id=1, source_target_pairs={{7,0},{0,1},{1,2},{2,3},{3,4},{4,5},{5,6},{6,7},{15,8},{8,9},{9,10... | collective-permute-start | bytes 1572872 | tf_op jit(solution)/shard_map/ppermute | solution.py:14
  133.9 30.3 %collective-permute-start.2 = (bf16[16,16,512]{2,1,0:T(8,128)(2,1)S(1)}, bf16[16,16,512]{2,1,0:T(8,128)(2,1)S(1)}, u32[]{:S(2)}, u32[]{:S(2)}) collective-permute-start(bf16[16,16,512]{2,1,0:T(8,128)(2,1)S(1)} %fusion.46), channel_id=1, source_target_pairs={{7,0},{0,1},{1,2},{2,3},{3,4},{4,5},{5,6},{6,7},{15,8},{8,9},{9,10... | collective-permute-start | bytes 786440 | tf_op jit(solution)/shard_map/ppermute | solution.py:14
Sparse Core Ops, SparseCore 0:
  10.2 58.8 all-gather.2
  71.3 36.7 all-gather.4
  112.4 70.6 reduce-scatter.4
  188.0 84.2 reduce-scatter.2
where the time goes:
time: 279 us
  waiting for transfers between devices  202 us (72%)
  matrix products  32.9 us (12%)
  between operations  20.9 us (7%)
  starting transfers between devices  10.1 us (4%)
  other arithmetic  7.93 us (3%)
  local copies, waits for them, and re-layouts  4.47 us (2%)
    reduce_scatter x1, waiting for transfers between devices, body(): lax.psum_scatter(term_in, ('fsdp', 'rows'), scatter_dimension=0, tiled=True)  89.1 us
    ppermute x5, waiting for transfers between devices, shifted(): return lax.ppermute(block, axis, route)  46.7 us
    all_gather x1, waiting for transfers between devices, body(): lax.all_gather(projection_out, ('fsdp', 'rows'), axis=0, tiled=True)  27.2 us
    all_gather x1, waiting for transfers between devices, body(): lax.all_gather(projection_in, ('fsdp', 'rows'), axis=0, tiled=True)  22.2 us
    reduce_scatter x1, waiting for transfers between devices, body(): lax.psum_scatter(term_out, ('fsdp', 'rows'), scatter_dimension=0, tiled=T...  16.6 us
    ppermute x5, starting transfers between devices, shifted(): return lax.ppermute(block, axis, route)  9.92 us
  transfers between devices with their start and end apart: 9, of which 6 were waited for; matrix products, arithmetic and copies ran while one was open for 16% of the time, Pallas kernels for 0%

commit v1 on v0

--- a/solution.py
+++ b/solution.py
@@ -6,6 +6,18 @@
 HEADS = 8
 HD = 64
 WIN = 16
+
+
+def gather_by_bits(x, axis, dim):
+    ways, here = (lax.axis_size(axis), lax.axis_index(axis))
+    grown, reach = (x, 1)
+    while reach < ways:
+        theirs = lax.ppermute(grown, axis, [(d, d ^ reach) for d in range(ways)])
+        mine_first = jnp.concatenate([grown, theirs], axis=dim)
+        theirs_first = jnp.concatenate([theirs, grown], axis=dim)
+        grown = jnp.where(here & reach == 0, mine_first, theirs_first)
+        reach = 2 * reach
+    return grown
 
 
 def shifted(block, axis, distance):
@@ -51,7 +63,7 @@
     shift_col = shifts[1]
     full_in, full_out = (
         lax.all_gather(projection_in, ("fsdp", "rows"), axis=0, tiled=True),
-        lax.all_gather(projection_out, ("fsdp", "rows"), axis=0, tiled=True),
+        gather_by_bits(projection_out, ("fsdp", "rows"), 0),
     )
     mask_wire = cell_mask.astype(jnp.bfloat16)
     next_tokens, next_mask = shifted((tokens, mask_wire), "rows", -1)

time: 279 us -> 238 us (0.85)
  waiting for transfers between devices: 202 us -> 151 us
  starting transfers between devices: 10.1 us -> 13.7 us
  matrix products: 32.9 us -> 36.1 us
  other arithmetic: 7.93 us -> 11.1 us
    all_gather x1 -> x0, waiting for transfers between devices: 27.2 us -> none  [body(): lax.all_gather(projection_out, ('fsdp', 'rows'), axis=0, tiled=True)]
    ppermute x0 -> x4, waiting for transfers between devices: none -> 19.9 us  [gather_by_bits(): theirs = lax.ppermute(grown, axis, [(d, d ^ reach) for d in range(ways)])]
    reduce_scatter x1, waiting for transfers between devices: 16.6 us -> 0.01 us  [body(): lax.psum_scatter(term_out, ('fsdp', 'rows'), scatter_dimension=0, tiled=T...]
    reduce_scatter x1, waiting for transfers between devices: 89.1 us -> 74.3 us  [body(): lax.psum_scatter(term_in, ('fsdp', 'rows'), scatter_dimension=0, tiled=True)]
    ppermute x5, waiting for transfers between devices: 46.7 us -> 33.7 us  [shifted(): return lax.ppermute(block, axis, route)]
    ppermute x0 -> x4, starting transfers between devices: none -> 4.79 us  [gather_by_bits(): theirs = lax.ppermute(grown, axis, [(d, d ^ reach) for d in range(ways)])]
    select_n x0 -> x3, other arithmetic: none -> 3.07 us  [gather_by_bits(): grown = jnp.where(here & reach == 0, mine_first, theirs_first)]
  transfers between devices with their start and end apart: 9 -> 12, of which waited for: 6 -> 9; matrix products, arithmetic and copies ran while one was open for 16% -> 17% of each run, Pallas kernels for 0% -> 0%
where the time goes in v1:
time: 238 us
  waiting for transfers between devices  151 us (63%)
  matrix products  36.1 us (15%)
  between operations  21.2 us (9%)
  starting transfers between devices  13.7 us (6%)
  other arithmetic  11.1 us (5%)
  local copies, waits for them, and re-layouts  4.79 us (2%)
    reduce_scatter x1, waiting for transfers between devices, body(): lax.psum_scatter(term_in, ('fsdp', 'rows'), scatter_dimension=0, tiled=True)  74.3 us
    ppermute x5, waiting for transfers between devices, shifted(): return lax.ppermute(block, axis, route)  33.7 us
    all_gather x1, waiting for transfers between devices, body(): lax.all_gather(projection_in, ('fsdp', 'rows'), axis=0, tiled=True)  22.1 us
    ppermute x4, waiting for transfers between devices, gather_by_bits(): theirs = lax.ppermute(grown, axis, [(d, d ^ reach) for d in range(ways)])  19.9 us
    ppermute x5, starting transfers between devices, shifted(): return lax.ppermute(block, axis, route)  8.76 us
    dot_general x1, matrix products, body(): jnp.einsum('whqk,wkhd->wqhd', grad_scores, key_heads, preferred_element_t...  4.99 us
    dot_general x1, matrix products, body(): jnp.einsum('whqk,wqhd->wkhd', grad_scores, query_heads, preferred_element...  4.98 us
    ppermute x4, starting transfers between devices, gather_by_bits(): theirs = lax.ppermute(grown, axis, [(d, d ^ reach) for d in range(ways)])  4.79 us
  transfers between devices with their start and end apart: 12, of which 9 were waited for; matrix products, arithmetic and copies ran while one was open for 17% of the time, Pallas kernels for 0%

profile of v1, /device:TPU:0, one launch (start us, length us, event | category | flops | bytes accessed | tf_op | source)
XLA Modules:
  0.0 237.6 jit_solution(4126988125569818146)
XLA Ops:
  8.6 6.0 %collective-permute-start.1 = (bf16[1,16,16]{2,1,0:T(8,128)(2,1)S(1)}, bf16[1,16,16]{2,1,0:T(8,128)(2,1)S(1)}, u32[]{:S(2)}, u32[]{:S(2)}) collective-permute-start(bf16[1,16,16]{2,1,0:T(8,128)(2,1)S(1)} %convert_element_type.146), channel_id=1, source_target_pairs={{1,0},{2,1},{3,2},{4,3},{5,4},{6,5},{7,6},{0,7},{9,8},{10,9},{11,1... | collective-permute-start | bytes 1544 | tf_op jit(solution)/shard_map/ppermute | solution.py:26
  15.2 1.4 collective-permute-start
  16.6 1.4 fusion.67
  25.1 18.8 %collective-permute-done = bf16[1,16,16,1024]{3,2,1,0:T(8,128)(2,1)S(1)} collective-permute-done((bf16[1,16,16,1024]{3,2,1,0:T(8,128)(2,1)}, bf16[1,16,16,1024]{3,2,1,0:T(8,128)(2,1)S(1)}, u32[]{:S(2)}, u32[]{:S(2)}) %collective-permute-start) | collective-permute-done | bytes 524320 | tf_op jit(solution)/shard_map/ppermute | solution.py:26
  44.0 1.2 fusion.39
  47.0 22.1 %all-gather.2.cloned.1.call-done = bf16[1024,1536]{1,0:T(8,128)(2,1)} async-done(((bf16[64,1536]{1,0:T(8,128)(2,1)}), bf16[1024,1536]{1,0:T(8,128)(2,1)}) %all-gather.2.cloned.1.call-update) | async-done | bytes 3145744 | tf_op jit(solution)/shard_map/all_gather | solution.py:65
  69.1 3.7 %convolution_convert_fusion = bf16[256,1536]{1,0:T(8,128)(2,1)} fusion(bf16[256,1024]{1,0:T(8,128)(2,1)S(1)} %fusion.29, bf16[1024,1536]{1,0:T(8,128)(2,1)} %all-gather.2.cloned.1.call-done), kind=kOutput, calls=%fused_computation.2 | convolution fusion | flops 805699584 | bytes 4456448 | tf_op jit(solution)/shard_map/dot_general | solution.py:99
  72.8 1.4 copy.21
  74.2 2.2 fusion.68
  76.4 1.9 convolution_convert_fusion.2
  78.4 1.8 fusion.69
  80.8 3.7 %collective-permute-done.3 = bf16[32,1024]{1,0:T(8,128)(2,1)S(1)} collective-permute-done((bf16[32,1024]{1,0:T(8,128)(2,1)S(1)}, bf16[32,1024]{1,0:T(8,128)(2,1)S(1)}, u32[]{:S(2)}, u32[]{:S(2)}) %collective-permute-start.3) | collective-permute-done | bytes 65568 | tf_op jit(solution)/shard_map/ppermute | solution.py:15
  84.6 2.0 collective-permute-start.4
  86.5 3.2 %collective-permute-done.4 = bf16[64,1024]{1,0:T(8,128)(2,1)} collective-permute-done((bf16[64,1024]{1,0:T(8,128)(2,1)S(1)}, bf16[64,1024]{1,0:T(8,128)(2,1)}, u32[]{:S(2)}, u32[]{:S(2)}) %collective-permute-start.4) | collective-permute-done | bytes 131104 | tf_op jit(solution)/shard_map/ppermute | solution.py:15
  89.7 1.0 maximum_select_fusion.2
  90.8 2.2 collective-permute-start.5
  93.0 10.8 %collective-permute-done.5 = bf16[128,1024]{1,0:T(8,128)(2,1)} collective-permute-done((bf16[128,1024]{1,0:T(8,128)(2,1)S(1)}, bf16[128,1024]{1,0:T(8,128)(2,1)}, u32[]{:S(2)}, u32[]{:S(2)}) %collective-permute-start.5) | collective-permute-done | bytes 262176 | tf_op jit(solution)/shard_map/ppermute | solution.py:15
  103.8 2.0 maximum_select_fusion.1
  105.8 2.2 collective-permute-done.6
  108.0 2.8 %convolution_convert_fusion.1 = bf16[256,512]{1,0:T(8,128)(2,1)} fusion(bf16[256,1024]{1,0:T(8,128)(2,1)S(1)} %bitcast.110, bf16[256,1024]{1,0:T(8,128)(2,1)} %collective-permute-done.6, bf16[256,1024]{1,0:T(8,128)(2,1)} %maximum_select_fusion.1, pred[]{:T(512)S(6)} %eq.46), kind=kOutput, calls=%fused_computation.18 | convolution fusion | flops 273285120 | bytes 1835009 | tf_op jit(solution)/shard_map/dot_general | solution.py:132
  110.8 1.1 copy.24
  111.9 1.8 fusion.49
  113.7 5.0 %fusion.14 = bf16[1,256,1,8,64]{1,4,3,2,0:T(8,128)(2,1)} fusion(f32[8,256,256]{1,2,0:T(8,128)} %fusion.49, bf16[1,256,3,8,64]{1,4,3,2,0:T(8,128)(2,1)S(1)} %bitcast.117, f32[8,256,256]{1,2,0:T(8,128)} %get-tuple-element.11, f32[8,256]{1,0:T(8,128)S(1)} %get-tuple-element.10), kind=kOutput, calls=%fused_computation.15 | convolution fusion | flops 70781184 | bytes 8929280 | tf_op jit(solution)/shard_map/whqk,wkhd->wqhd/dot_general | solution.py:147
  118.7 5.0 %fusion.17 = bf16[1,256,1,8,64]{1,4,3,2,0:T(8,128)(2,1)} fusion(f32[8,256,256]{1,2,0:T(8,128)} %fusion.49, bf16[1,256,3,8,64]{1,4,3,2,0:T(8,128)(2,1)S(1)} %bitcast.118, f32[8,256,256]{1,2,0:T(8,128)} %get-tuple-element.11, f32[8,256]{1,0:T(8,128)S(1)} %get-tuple-element.10), kind=kOutput, calls=%fused_computation.16 | convolution fusion | flops 70781184 | bytes 8929280 | tf_op jit(solution)/shard_map/whqk,wqhd->wkhd/dot_general | solution.py:150
  123.6 2.1 convolution_bitcast_fusion
  125.9 3.8 %fusion.31 = f32[1024,1536]{1,0:T(8,128)} fusion(bf16[256,1536]{0,1:T(8,128)(2,1)S(1)} %bitcast.111, f32[1,256,1,1,1,1,1024]{6,1,5,4,3,2,0:T(8,128)S(1)} %bitcast.108, f32[256]{0:T(256)S(1)} %add_rsqrt_fusion, f32[256]{0:T(256)S(1)} %div.24), kind=kOutput, calls=%fused_computation.51 | convolution fusion | flops 806092800 | bytes 8128512 | tf_op jit(solution)/shard_map/dot_general | solution.py:161
  132.6 3.1 %fusion.65 = (f32[256]{0:T(256)S(1)}, f32[256]{0:T(256)S(1)}, f32[256,1024]{1,0:T(8,128)S(1)}) fusion(f32[256]{0:T(256)S(1)} %add_rsqrt_fusion, f32[256]{0:T(256)S(1)} %div.24, bf16[16,16,1024]{2,1,0:T(8,128)(2,1)S(1)} %get-tuple-element.7, bf16[256,1536]{0,1:T(8,128)(2,1)S(1)} %bitcast.112, bf16[1024,1536]{1,0:T(8,128)(2,1)} %all-gather.2.cloned.1.call-done), kind=kOutput, calls=%fused_computation.111 | convolution fusion | flops 806878720 | bytes 5509120 | tf_op jit(solution)/shard_map/dot_general | solution.py:164
  138.0 7.1 %collective-permute-done.2 = bf16[16,16,512]{2,1,0:T(8,128)(2,1)S(1)} collective-permute-done((bf16[16,16,512]{2,1,0:T(8,128)(2,1)S(1)}, bf16[16,16,512]{2,1,0:T(8,128)(2,1)S(1)}, u32[]{:S(2)}, u32[]{:S(2)}) %collective-permute-start.2) | collective-permute-done | bytes 262176 | tf_op jit(solution)/shard_map/ppermute | solution.py:26
  145.1 2.9 %fusion.13 = bf16[1,16,16,1024]{3,2,1,0:T(8,128)(2,1)} fusion(s32[]{:T(128)S(6)} %select_n.80, bf16[16,16,512]{2,1,0:T(8,128)(2,1)S(1)} %collective-permute-done.2, bf16[16,16,512]{2,1,0:T(8,128)(2,1)S(1)} %fusion.46, bf16[256,1024]{1,0:T(8,128)(2,1)} %collective-permute-done.6, bf16[256,1024]{1,0:T(8,128)(2,1)} %maximum_select_fusion.1, pred[]{:T(512)S(6)} %eq.46, ...), kind=kOutput, calls=%fused_computation.14 | convolution fusion | flops 274071552 | bytes 2621445 | tf_op jit(solution)/shard_map/dot_general | solution.py:122
  148.0 7.8 %collective-permute-done.8 = bf16[16,16,1024]{2,1,0:T(8,128)(2,1)S(1)} collective-permute-done((bf16[16,16,1024]{2,1,0:T(8,128)(2,1)S(1)}, bf16[16,16,1024]{2,1,0:T(8,128)(2,1)S(1)}, u32[]{:S(2)}, u32[]{:S(2)}) %collective-permute-start.8) | collective-permute-done | bytes 524320 | tf_op jit(solution)/shard_map/ppermute | solution.py:26
  155.8 1.0 fusion.34
  156.8 74.3 %reduce-scatter.3.cloned.1.call-done = f32[64,1536]{1,0:T(8,128)} async-done(((f32[1024,1536]{1,0:T(8,128)}), f32[64,1536]{1,0:T(8,128)}) %reduce-scatter.3.cloned.1.call-update) | async-done | bytes 393232 | tf_op jit(solution)/shard_map/reduce_scatter | solution.py:181
  (51 shorter events, 9.7 us)
Async XLA Ops:
  7.2 61.9 %all-gather.2.cloned.1.call-start = ((), (), s32[]{:S(2)}) async-start(), calls=%async_computation.2 | async-start | bytes 3342336 | tf_op jit(solution)/shard_map/all_gather | solution.py:65
  7.9 148.9 %reduce-scatter.5.cloned.1.call-start = ((), (), s32[]{:S(2)}) async-start(), calls=%async_computation.4 | async-start | bytes 2228224 | tf_op jit(solution)/shard_map/reduce_scatter | solution.py:182
  8.6 16.1 %collective-permute-start.1 = (bf16[1,16,16]{2,1,0:T(8,128)(2,1)S(1)}, bf16[1,16,16]{2,1,0:T(8,128)(2,1)S(1)}, u32[]{:S(2)}, u32[]{:S(2)}) collective-permute-start(bf16[1,16,16]{2,1,0:T(8,128)(2,1)S(1)} %convert_element_type.146), channel_id=1, source_target_pairs={{1,0},{2,1},{3,2},{4,3},{5,4},{6,5},{7,6},{0,7},{9,8},{10,9},{11,1... | collective-permute-start | bytes 1544 | tf_op jit(solution)/shard_map/ppermute | solution.py:26
  14.7 31.2 %collective-permute-start.7 = (bf16[1,16,16,1024]{3,2,1,0:T(8,128)(2,1)}, bf16[1,16,16,1024]{3,2,1,0:T(8,128)(2,1)S(1)}, u32[]{:S(2)}, u32[]{:S(2)}) collective-permute-start(bf16[1,16,16,1024]{3,2,1,0:T(8,128)(2,1)} %param.11), channel_id=1, source_target_pairs={{1,0},{2,1},{3,2},{4,3},{5,4},{6,5},{7,6},{0,7},{9,8},{10,9},{11,1... | collective-permute-start | bytes 1572872 | tf_op jit(solution)/shard_map/ppermute | solution.py:26
  15.2 28.8 %collective-permute-start = (bf16[1,16,16,1024]{3,2,1,0:T(8,128)(2,1)}, bf16[1,16,16,1024]{3,2,1,0:T(8,128)(2,1)S(1)}, u32[]{:S(2)}, u32[]{:S(2)}) collective-permute-start(bf16[1,16,16,1024]{3,2,1,0:T(8,128)(2,1)} %param.6), channel_id=1, source_target_pairs={{1,0},{2,1},{3,2},{4,3},{5,4},{6,5},{7,6},{0,7},{9,8},{10,9},{11,1... | collective-permute-start | bytes 1572872 | tf_op jit(solution)/shard_map/ppermute | solution.py:26
  44.0 1.9 copy-start
  78.4 1.8 copy-start.4
  80.1 150.9 %reduce-scatter.3.cloned.1.call-start = ((), (), s32[]{:S(2)}) async-start(), calls=%async_computation.3 | async-start | bytes 6684672 | tf_op jit(solution)/shard_map/reduce_scatter | solution.py:181
  80.2 4.3 %collective-permute-start.3 = (bf16[32,1024]{1,0:T(8,128)(2,1)S(1)}, bf16[32,1024]{1,0:T(8,128)(2,1)S(1)}, u32[]{:S(2)}, u32[]{:S(2)}) collective-permute-start(bf16[32,1024]{1,0:T(8,128)(2,1)S(1)} %copy-done.4), channel_id=1, source_target_pairs={{0,1},{1,0},{2,3},{3,2},{4,5},{5,4},{6,7},{7,6},{8,9},{9,8},{10,11... | collective-permute-start | bytes 196616 | tf_op jit(solution)/shard_map/ppermute | solution.py:15
  84.6 5.1 %collective-permute-start.4 = (bf16[64,1024]{1,0:T(8,128)(2,1)S(1)}, bf16[64,1024]{1,0:T(8,128)(2,1)}, u32[]{:S(2)}, u32[]{:S(2)}) collective-permute-start(bf16[64,1024]{1,0:T(8,128)(2,1)S(1)} %maximum_select_fusion.5), channel_id=1, source_target_pairs={{0,2},{1,3},{2,0},{3,1},{4,6},{5,7},{6,4},{7,5},{8,10},{9,11},{10,... | collective-permute-start | bytes 393224 | tf_op jit(solution)/shard_map/ppermute | solution.py:15
  90.8 13.0 %collective-permute-start.5 = (bf16[128,1024]{1,0:T(8,128)(2,1)S(1)}, bf16[128,1024]{1,0:T(8,128)(2,1)}, u32[]{:S(2)}, u32[]{:S(2)}) collective-permute-start(bf16[128,1024]{1,0:T(8,128)(2,1)S(1)} %maximum_select_fusion.2), channel_id=1, source_target_pairs={{0,4},{1,5},{2,6},{3,7},{4,0},{5,1},{6,2},{7,3},{8,12},{9,13},{10,... | collective-permute-start | bytes 786440 | tf_op jit(solution)/shard_map/ppermute | solution.py:15
  105.8 2.3 collective-permute-start.6
  123.6 2.1 copy-start.2
  123.6 2.1 copy-start.3
  131.9 13.3 %collective-permute-start.2 = (bf16[16,16,512]{2,1,0:T(8,128)(2,1)S(1)}, bf16[16,16,512]{2,1,0:T(8,128)(2,1)S(1)}, u32[]{:S(2)}, u32[]{:S(2)}) collective-permute-start(bf16[16,16,512]{2,1,0:T(8,128)(2,1)S(1)} %fusion.46), channel_id=1, source_target_pairs={{7,0},{0,1},{1,2},{2,3},{3,4},{4,5},{5,6},{6,7},{15,8},{8,9},{9,10... | collective-permute-start | bytes 786440 | tf_op jit(solution)/shard_map/ppermute | solution.py:26
  135.8 9.4 %copy-start.1 = (bf16[1,16,16,1024]{3,2,1,0:T(8,128)(2,1)S(1)}, bf16[1,16,16,1024]{3,2,1,0:T(8,128)(2,1)}, u32[]{:S(2)}) copy-start(bf16[1,16,16,1024]{3,2,1,0:T(8,128)(2,1)} %param.6) | copy-start | bytes 1572868
  136.6 19.2 %collective-permute-start.8 = (bf16[16,16,1024]{2,1,0:T(8,128)(2,1)S(1)}, bf16[16,16,1024]{2,1,0:T(8,128)(2,1)S(1)}, u32[]{:S(2)}, u32[]{:S(2)}) collective-permute-start(bf16[16,16,1024]{2,1,0:T(8,128)(2,1)S(1)} %fusion.35), channel_id=1, source_target_pairs={{7,0},{0,1},{1,2},{2,3},{3,4},{4,5},{5,6},{6,7},{15,8},{8,9},{9,10... | collective-permute-start | bytes 1572872 | tf_op jit(solution)/shard_map/ppermute | solution.py:26
Sparse Core Ops, SparseCore 0:
  10.2 58.8 all-gather.1
  80.3 60.4 reduce-scatter.4
  145.8 85.2 reduce-scatter.2
